TPU v7x, 32 devices: a whole 2x2x4 slice. The times are simulated.
32 devices in a mesh: groups: 2 (over x), label: 8 (over z, y), cent: 2 (over core).
Axes of the slice: x: 2, y: 2, z: 4, core: 2. Of those that a mesh axis runs over, the one named last changes fastest.
Arguments:
- embeddings: bfloat16 [768, 16384], P('label', 'groups'), parts along dimension 1, may hold values from -40 to 40
- centroids: bfloat16 [2, 8192, 768], P('cent', ('groups', 'label')), parts along dimension 1, may hold values from -1 to 1
Outputs:
- new_centroids: float32 [2, 8192, 768], P('cent', ('groups', 'label')), parts along dimension 1
There are 2 independent parts, one for each index of `groups`. A program takes and returns all parts, laid end to end along the dimension named above; each array names one. Nothing has to cross between parts.
All inputs are finite; a program needn't handle non-finite values.
Results may differ from a plain program's by a relative error of at most 0.012.
Values may be sent and summed in bfloat16 or wider, within the bound.
A program may use at most 128 MiB of HBM per device.

v0:
```python
import jax
import jax.numpy as jnp
from jax import lax
from jax.sharding import PartitionSpec as P

prior_weight = 1.0


def weights_cent(scores):
    row_top = lax.pmax(jnp.max(scores, axis=1), "cent")
    exponent = jnp.exp(scores - row_top[:, None])
    row_sum = lax.psum(jnp.sum(exponent, axis=1), "cent")
    return (exponent / row_sum[:, None]).astype(jnp.bfloat16)


def score_against(feature_table, centroid_slice):
    half_norms = 0.5 * jnp.sum(jnp.square(centroid_slice.astype(jnp.float32)), axis=1)
    products = lax.dot_general(
        feature_table, centroid_slice, (((0,), (1,)), ((), ())), preferred_element_type=jnp.float32
    )
    return products - half_norms[None, :]


def weighted_sums(weights, feature_table):
    partial_terms = lax.dot_general(
        weights, feature_table, (((0,), (1,)), ((), ())), preferred_element_type=jnp.float32
    )
    counts = jnp.sum(weights, axis=0, dtype=jnp.float32)
    return (partial_terms, counts)


def body(embeddings, centroids):
    held_centroids = centroids[0]
    relaid = lax.all_to_all(embeddings, "label", split_axis=1, concat_axis=0, tiled=True)
    scores = score_against(relaid, lax.all_gather(centroids, "label", axis=1, tiled=True)[0])
    weights = weights_cent(scores)
    partial_terms, counts = weighted_sums(weights, relaid)
    numerators, totals = (
        lax.psum_scatter(
            partial_terms.astype(jnp.bfloat16), "label", scatter_dimension=0, tiled=True
        ).astype(jnp.float32),
        lax.psum_scatter(
            counts.astype(jnp.bfloat16), "label", scatter_dimension=0, tiled=True
        ).astype(jnp.float32),
    )
    updated = (numerators + prior_weight * held_centroids.astype(jnp.float32)) / (
        totals + prior_weight
    )[:, None]
    return updated[None]


def solution(mesh):
    return jax.shard_map(
        body,
        mesh=mesh,
        in_specs=(P("label", "groups"), P("cent", ("groups", "label"), None)),
        out_specs=P("cent", ("groups", "label"), None),
        check_vma=False,
    )
```

profile of v0, /device:TPU:0, one launch (start us, length us, event | category | flops | bytes accessed | tf_op | source)
XLA Modules:
  0.0 312.0 jit_solution(1574253930327543209)
XLA Ops:
  6.5 0.0 all-gather.2.cloned.1.call-start
  6.5 0.7 all-gather.2.cloned.1.call-update
  7.3 2.7 copy.7
  10.0 7.3 %all-to-all-start = ((bf16[96,8,1024]{2,0,1:T(8,128)(2,1)}), bf16[96,8,1024]{2,0,1:T(8,128)(2,1)S(1)}, u32[]{:S(2)}, u32[]{:S(2)}) async-start(bf16[96,8,1024]{2,0,1:T(8,128)(2,1)} %bitcast.21), calls=%async_computation | async-start | bytes 3145728 | tf_op jit(solution)/shard_map/all_to_all | solution.py:34
  17.3 0.0 reduce-scatter.2.cloned.1.call-start
  17.3 121.1 %all-gather.2.cloned.1.call-done = bf16[1,4096,768]{2,1,0:T(8,128)(2,1)} async-done(((bf16[1,512,768]{2,1,0:T(8,128)(2,1)}), bf16[1,4096,768]{2,1,0:T(8,128)(2,1)}) %all-gather.2.cloned.1.call-update) | async-done | bytes 6291472 | tf_op jit(solution)/shard_map/all_gather | solution.py:35
  138.4 4.1 %multiply_reduce_fusion = f32[4096]{0:T(1024)S(1)} fusion(bf16[1,4096,768]{2,1,0:T(8,128)(2,1)} %all-gather.2.cloned.1.call-done), kind=kLoop, calls=%fused_computation.4 | loop fusion | flops 9433088 | bytes 6307840 | tf_op jit(solution)/shard_map/reduce_sum | solution.py:17
  142.5 0.0 all-to-all-done
  142.6 13.1 %subtract_reduce_fusion = (f32[1024]{0:T(1024)S(1)}, f32[1024,4096]{1,0:T(8,128)}) fusion(f32[4096]{0:T(1024)S(1)} %broadcast_multiply_fusion, bf16[768,1024]{1,0:T(8,128)(2,1)S(1)} %bitcast.23, bf16[1,4096,768]{2,1,0:T(8,128)(2,1)} %all-gather.2.cloned.1.call-done), kind=kOutput, calls=%fused_computation.2 | convolution fusion | flops 6450838528 | bytes 24662016 | tf_op jit(solution)/shard_map/dot_general | solution.py:18
  155.6 2.4 pmax.7
  158.1 8.6 %fusion = f32[1024]{0:T(1024)S(1)} fusion(f32[1024,4096]{1,0:T(8,128)} %get-tuple-element.8, f32[1024]{0:T(1024)S(1)} %pmax.7, f32[4096]{0:T(1024)S(1)} %broadcast_multiply_fusion), kind=kLoop, calls=%fused_computation.3 | loop fusion | flops 12581888 | bytes 16801792 | tf_op jit(solution)/shard_map/reduce_sum | solution.py:12
  166.7 2.5 psum.7
  169.2 8.1 %fusion.5 = (bf16[4096]{0:T(1024)(128)(2,1)S(1)}, bf16[1024,4096]{1,0:T(8,128)(2,1)S(1)}) fusion(f32[1024]{0:T(1024)S(1)} %psum.7, f32[1024]{0:T(1024)S(1)} %pmax.7, f32[1024,4096]{1,0:T(8,128)} %get-tuple-element.8, f32[4096]{0:T(1024)S(1)} %broadcast_multiply_fusion), kind=kLoop, calls=%fused_computation.14 | loop fusion | flops 20967424 | bytes 25198592 | tf_op jit(solution)/shard_map/reduce_sum | solution.py:28
  177.2 0.0 copy-start.1
  177.3 0.0 copy-start
  177.3 9.0 %convolution_convert_fusion = bf16[4096,768]{1,0:T(8,128)(2,1)} fusion(bf16[1024,4096]{1,0:T(8,128)(2,1)S(1)} %get-tuple-element.6, bf16[768,1024]{1,0:T(8,128)(2,1)S(1)} %bitcast.24), kind=kOutput, calls=%fused_computation.5 | convolution fusion | flops 6445596672 | bytes 16252928 | tf_op jit(solution)/shard_map/dot_general | solution.py:25
  186.2 0.0 reduce-scatter.2.cloned.1.call-update
  186.3 0.0 copy-done.1
  186.3 0.6 dynamic-slice
  187.5 19.7 %all-reduce = bf16[4096]{0:T(1024)(128)(2,1)S(1)} all-reduce(bf16[4096]{0:T(1024)(128)(2,1)S(1)} %get-tuple-element.5), channel_id=3, replica_groups=mesh['groups'=2,'label'=8,'cent'=2] {'label'}, use_global_device_ids=true, to_apply=%region_7.0.clone | all-reduce | flops 4096 | bytes 16384
  207.3 0.1 convert_add_fusion.1
  207.3 95.3 %reduce-scatter.2.cloned.1.call-done = bf16[512,768]{1,0:T(8,128)(2,1)} async-done(((bf16[4096,768]{1,0:T(8,128)(2,1)}), bf16[512,768]{1,0:T(8,128)(2,1)}) %reduce-scatter.2.cloned.1.call-update) | async-done | bytes 786448 | tf_op jit(solution)/shard_map/reduce_scatter | solution.py:39
  302.6 0.0 copy-done
  302.6 2.5 fusion.4
  (1 shorter events, 0.0 us)
Async XLA Ops:
  6.5 131.9 %all-gather.2.cloned.1.call-start = ((), (), s32[]{:S(2)}) async-start(), calls=%async_computation.2 | async-start | bytes 7077888 | tf_op jit(solution)/shard_map/all_gather | solution.py:35
  10.0 132.6 %all-to-all-start = ((bf16[96,8,1024]{2,0,1:T(8,128)(2,1)}), bf16[96,8,1024]{2,0,1:T(8,128)(2,1)S(1)}, u32[]{:S(2)}, u32[]{:S(2)}) async-start(bf16[96,8,1024]{2,0,1:T(8,128)(2,1)} %bitcast.21), calls=%async_computation | async-start | bytes 3145728 | tf_op jit(solution)/shard_map/all_to_all | solution.py:34
  17.3 285.4 %reduce-scatter.2.cloned.1.call-start = ((), (), s32[]{:S(2)}) async-start(), calls=%async_computation.3 | async-start | bytes 7077888 | tf_op jit(solution)/shard_map/reduce_scatter | solution.py:39
  177.2 9.0 %copy-start.1 = (u32[32]{0:T(128)S(1)}, u32[32]{0:T(128)}, u32[]{:S(2)}) copy-start(u32[32]{0:T(128)} %constant.13) | copy-start | bytes 388
  177.3 125.4 %copy-start = (bf16[1,512,768]{2,1,0:T(8,128)(2,1)S(1)}, bf16[1,512,768]{2,1,0:T(8,128)(2,1)}, u32[]{:S(2)}) copy-start(bf16[1,512,768]{2,1,0:T(8,128)(2,1)} %param.3) | copy-start | bytes 2359300
Sparse Core Ops, SparseCore 0:
  9.5 128.8 all-gather.1
  186.4 116.2 reduce-scatter.1
where the time goes:
time: 312 us
  waiting for transfers between devices  217 us (70%)
  blocking collectives  24.6 us (8%)
  other arithmetic  23.4 us (8%)
  matrix products  22 us (7%)
  between operations  14.1 us (5%)
  starting transfers between devices  7.32 us (2%)
  local copies, waits for them, and re-layouts  3.31 us (1%)
    all_gather x1, waiting for transfers between devices, body(): lax.all_gather(centroids, 'label', axis=1, tiled=True)[0]  121 us
    reduce_scatter x1, waiting for transfers between devices, body(): lax.psum_scatter(partial_terms.astype(jnp.bfloat16), 'label', scatter_dim...  95.3 us
    unnamed x1, blocking collectives  19.7 us
    dot_general x1, matrix products, score_against(): lax.dot_general(feature_table, centroid_slice, (((0,), (1,)), ((), ())),...  13.1 us
    dot_general x1, matrix products, weighted_sums(): lax.dot_general(weights, feature_table, (((0,), (1,)), ((), ())), preferr...  8.97 us
    reduce_sum x1, other arithmetic, weights_cent(): row_sum = lax.psum(jnp.sum(exponent, axis=1), 'cent')  8.64 us
    reduce_sum x1, other arithmetic, weighted_sums(): counts = jnp.sum(weights, axis=0, dtype=jnp.float32)  8.07 us
    all_to_all x1, starting transfers between devices, body(): lax.all_to_all(embeddings, 'label', split_axis=1, concat_axis=0, tiled=True)  7.28 us
  transfers between devices with their start and end apart: 3, of which 2 were waited for; matrix products, arithmetic and copies ran while one was open for 2% of the time, Pallas kernels for 0%

commit v1 on v0

--- a/solution.py
+++ b/solution.py
@@ -31,7 +31,19 @@
 
 def body(embeddings, centroids):
     held_centroids = centroids[0]
-    relaid = lax.all_to_all(embeddings, "label", split_axis=1, concat_axis=0, tiled=True)
+    ways, here = (lax.axis_size("label"), lax.axis_index("label"))
+    width = embeddings.shape[1] // ways
+    shape = list(embeddings.shape)
+    shape[1] = width
+    height = shape[0]
+    shape[0] = height * ways
+    full = jnp.zeros(shape, embeddings.dtype)
+    for mask in range(ways):
+        part = lax.dynamic_slice_in_dim(embeddings, (here ^ mask) * width, width, axis=1)
+        if mask:
+            part = lax.ppermute(part, "label", [(d, d ^ mask) for d in range(ways)])
+        full = lax.dynamic_update_slice_in_dim(full, part, (here ^ mask) * height, axis=0)
+    relaid = full
     scores = score_against(relaid, lax.all_gather(centroids, "label", axis=1, tiled=True)[0])
     weights = weights_cent(scores)
     partial_terms, counts = weighted_sums(weights, relaid)

time: 312 us -> 310 us (level)
  starting transfers between devices: 7.32 us -> 12.5 us
  waiting for transfers between devices: 217 us -> 213 us
    all_gather x1, waiting for transfers between devices: 121 us -> 81.2 us  [body(): lax.all_gather(centroids, 'label', axis=1, tiled=True)[0]]
    ppermute x0 -> x7, waiting for transfers between devices: none -> 35.9 us  [body(): part = lax.ppermute(part, 'label', [(d, d ^ mask) for d in range(ways)])]
    ppermute x0 -> x7, starting transfers between devices: none -> 12.4 us  [body(): part = lax.ppermute(part, 'label', [(d, d ^ mask) for d in range(ways)])]
    all_to_all x1 -> x0, starting transfers between devices: 7.28 us -> none  [body(): lax.all_to_all(embeddings, 'label', split_axis=1, concat_axis=0, tiled=True)]
  transfers between devices with their start and end apart: 3 -> 9, of which waited for: 2 -> 6; matrix products, arithmetic and copies ran while one was open for 2% -> 1% of each run, Pallas kernels for 0% -> 0%
where the time goes in v1:
time: 310 us
  waiting for transfers between devices  213 us (69%)
  blocking collectives  24.7 us (8%)
  other arithmetic  23.5 us (8%)
  matrix products  19.2 us (6%)
  between operations  14.2 us (5%)
  starting transfers between devices  12.5 us (4%)
  local copies, waits for them, and re-layouts  3.23 us (1%)
    reduce_scatter x1, waiting for transfers between devices, body(): lax.psum_scatter(partial_terms.astype(jnp.bfloat16), 'label', scatter_dim...  94.8 us
    all_gather x1, waiting for transfers between devices, body(): lax.all_gather(centroids, 'label', axis=1, tiled=True)[0]  81.2 us
    ppermute x7, waiting for transfers between devices, body(): part = lax.ppermute(part, 'label', [(d, d ^ mask) for d in range(ways)])  35.9 us
    unnamed x1, blocking collectives  19.8 us
    ppermute x7, starting transfers between devices, body(): part = lax.ppermute(part, 'label', [(d, d ^ mask) for d in range(ways)])  12.4 us
    dot_general x1, matrix products, score_against(): lax.dot_general(feature_table, centroid_slice, (((0,), (1,)), ((), ())),...  10.2 us
    dot_general x1, matrix products, weighted_sums(): lax.dot_general(weights, feature_table, (((0,), (1,)), ((), ())), preferr...  8.97 us
    reduce_sum x1, other arithmetic, weights_cent(): row_sum = lax.psum(jnp.sum(exponent, axis=1), 'cent')  8.64 us
  transfers between devices with their start and end apart: 9, of which 6 were waited for; matrix products, arithmetic and copies ran while one was open for 1% of the time, Pallas kernels for 0%

profile of v1, /device:TPU:0, one launch (start us, length us, event | category | flops | bytes accessed | tf_op | source)
XLA Modules:
  0.0 309.9 jit_solution(10795879948002125877)
XLA Ops:
  6.5 0.0 copy-start.2
  6.5 0.0 all-gather.2.cloned.1.call-start
  6.5 0.7 all-gather.2.cloned.1.call-update
  7.3 0.0 reduce-scatter.2.cloned.1.call-start
  7.3 0.2 broadcast_in_dim.4
  7.5 0.4 copy-done.2
  7.9 1.0 constant_dynamic-slice_fusion
  8.9 3.0 collective-permute-start
  11.9 1.6 collective-permute-start.1
  13.5 0.0 collective-permute-start.2
  13.5 3.0 collective-permute-start.3
  16.4 1.3 collective-permute-start.4
  17.7 0.0 collective-permute-done
  17.7 3.6 %collective-permute-start.5 = (bf16[96,1024]{1,0:T(8,128)(2,1)S(1)}, bf16[96,1024]{1,0:T(8,128)(2,1)S(1)}, u32[]{:S(2)}, u32[]{:S(2)}) collective-permute-start(bf16[96,1024]{1,0:T(8,128)(2,1)S(1)} %get-tuple-element.14), channel_id=1, source_target_pairs={{0,12},{2,14},{4,8},{6,10},{8,4},{10,6},{12,0},{14,2},{1,13},{3,15... | collective-permute-start | bytes 589832 | tf_op jit(solution)/shard_map/ppermute | solution.py:44
  21.4 10.2 %collective-permute-done.1 = bf16[96,1024]{1,0:T(8,128)(2,1)S(1)} collective-permute-done((bf16[96,1024]{1,0:T(8,128)(2,1)}, bf16[96,1024]{1,0:T(8,128)(2,1)S(1)}, u32[]{:S(2)}, u32[]{:S(2)}) %collective-permute-start.1) | collective-permute-done | bytes 196640 | tf_op jit(solution)/shard_map/ppermute | solution.py:44
  31.5 0.0 collective-permute-start.6
  31.6 4.5 %collective-permute-done.2 = bf16[96,1024]{1,0:T(8,128)(2,1)S(1)} collective-permute-done((bf16[96,1024]{1,0:T(8,128)(2,1)}, bf16[96,1024]{1,0:T(8,128)(2,1)S(1)}, u32[]{:S(2)}, u32[]{:S(2)}) %collective-permute-start.2) | collective-permute-done | bytes 196640 | tf_op jit(solution)/shard_map/ppermute | solution.py:44
  36.1 0.0 collective-permute-done.3
  36.1 18.4 %collective-permute-done.4 = bf16[96,1024]{1,0:T(8,128)(2,1)S(1)} collective-permute-done((bf16[96,1024]{1,0:T(8,128)(2,1)}, bf16[96,1024]{1,0:T(8,128)(2,1)S(1)}, u32[]{:S(2)}, u32[]{:S(2)}) %collective-permute-start.4) | collective-permute-done | bytes 196640 | tf_op jit(solution)/shard_map/ppermute | solution.py:44
  54.5 0.0 collective-permute-done.5
  54.5 2.8 collective-permute-done.6
  57.4 81.2 %all-gather.2.cloned.1.call-done = bf16[1,4096,768]{2,1,0:T(8,128)(2,1)} async-done(((bf16[1,512,768]{2,1,0:T(8,128)(2,1)}), bf16[1,4096,768]{2,1,0:T(8,128)(2,1)}) %all-gather.2.cloned.1.call-update) | async-done | bytes 6291472 | tf_op jit(solution)/shard_map/all_gather | solution.py:47
  138.5 0.0 copy-start
  138.5 4.2 %multiply_reduce_fusion = f32[4096]{0:T(1024)S(1)} fusion(bf16[1,4096,768]{2,1,0:T(8,128)(2,1)} %all-gather.2.cloned.1.call-done), kind=kLoop, calls=%fused_computation.4 | loop fusion | flops 9433088 | bytes 6307840 | tf_op jit(solution)/shard_map/reduce_sum | solution.py:17
  142.8 0.3 copy-done
  143.1 10.2 %subtract_reduce_fusion = (f32[1024]{0:T(1024)S(1)}, f32[1024,4096]{1,0:T(8,128)}) fusion(f32[4096]{0:T(1024)S(1)} %broadcast_multiply_fusion, bf16[768,1024]{1,0:T(8,128)(2,1)S(1)} %constant_dynamic-update-slice_fusion.6, bf16[1,4096,768]{2,1,0:T(8,128)(2,1)S(1)} %copy-done), kind=kOutput, calls=%fused_computation.2 | convolution fusion | flops 6450838528 | bytes 24662016 | tf_op jit(solution)/shard_map/dot_general | solution.py:18
  153.4 2.4 pmax.7
  155.8 8.6 %fusion = f32[1024]{0:T(1024)S(1)} fusion(f32[1024,4096]{1,0:T(8,128)} %get-tuple-element.16, f32[1024]{0:T(1024)S(1)} %pmax.7, f32[4096]{0:T(1024)S(1)} %broadcast_multiply_fusion), kind=kLoop, calls=%fused_computation.3 | loop fusion | flops 12581888 | bytes 16801792 | tf_op jit(solution)/shard_map/reduce_sum | solution.py:12
  164.5 2.5 psum.7
  166.9 8.1 %fusion.5 = (bf16[4096]{0:T(1024)(128)(2,1)S(1)}, bf16[1024,4096]{1,0:T(8,128)(2,1)S(1)}) fusion(f32[1024]{0:T(1024)S(1)} %psum.7, f32[1024]{0:T(1024)S(1)} %pmax.7, f32[1024,4096]{1,0:T(8,128)} %get-tuple-element.16, f32[4096]{0:T(1024)S(1)} %broadcast_multiply_fusion), kind=kLoop, calls=%fused_computation.28 | loop fusion | flops 20967424 | bytes 25198592 | tf_op jit(solution)/shard_map/reduce_sum | solution.py:28
  175.0 9.0 %convolution_convert_fusion = bf16[4096,768]{1,0:T(8,128)(2,1)} fusion(bf16[1024,4096]{1,0:T(8,128)(2,1)S(1)} %get-tuple-element.6, bf16[768,1024]{1,0:T(8,128)(2,1)S(1)} %constant_dynamic-update-slice_fusion.6), kind=kOutput, calls=%fused_computation.5 | convolution fusion | flops 6445596672 | bytes 16252928 | tf_op jit(solution)/shard_map/dot_general | solution.py:25
  184.0 0.0 copy-start.3
  184.0 0.0 copy-start.1
  184.0 0.0 reduce-scatter.2.cloned.1.call-update
  184.0 0.6 copy-done.3
  184.6 0.6 dynamic-slice
  185.9 19.8 %all-reduce = bf16[4096]{0:T(1024)(128)(2,1)S(1)} all-reduce(bf16[4096]{0:T(1024)(128)(2,1)S(1)} %get-tuple-element.5), channel_id=3, replica_groups=mesh['groups'=2,'label'=8,'cent'=2] {'label'}, use_global_device_ids=true, to_apply=%region_7.0.clone | all-reduce | flops 4096 | bytes 16384
  205.6 0.1 convert_add_fusion.1
  205.7 94.8 %reduce-scatter.2.cloned.1.call-done = bf16[512,768]{1,0:T(8,128)(2,1)} async-done(((bf16[4096,768]{1,0:T(8,128)(2,1)}), bf16[512,768]{1,0:T(8,128)(2,1)}) %reduce-scatter.2.cloned.1.call-update) | async-done | bytes 786448 | tf_op jit(solution)/shard_map/reduce_scatter | solution.py:51
  300.5 0.0 copy-done.1
  300.5 2.5 fusion.4
  (8 shorter events, 0.1 us)
Async XLA Ops:
  6.5 1.4 copy-start.2
  6.5 132.0 %all-gather.2.cloned.1.call-start = ((), (), s32[]{:S(2)}) async-start(), calls=%async_computation.1 | async-start | bytes 7077888 | tf_op jit(solution)/shard_map/all_gather | solution.py:47
  7.3 293.3 %reduce-scatter.2.cloned.1.call-start = ((), (), s32[]{:S(2)}) async-start(), calls=%async_computation.2 | async-start | bytes 7077888 | tf_op jit(solution)/shard_map/reduce_scatter | solution.py:51
  8.9 8.8 %collective-permute-start = (bf16[96,1024]{1,0:T(8,128)(2,1)}, bf16[96,1024]{1,0:T(8,128)(2,1)S(1)}, u32[]{:S(2)}, u32[]{:S(2)}) collective-permute-start(bf16[96,1024]{1,0:T(8,128)(2,1)} %get-tuple-element.12), channel_id=1, source_target_pairs={{0,2},{2,0},{4,6},{6,4},{8,10},{10,8},{12,14},{14,12},{1,3},{3,1},... | collective-permute-start | bytes 589832 | tf_op jit(solution)/shard_map/ppermute | solution.py:44
  11.9 19.6 %collective-permute-start.1 = (bf16[96,1024]{1,0:T(8,128)(2,1)}, bf16[96,1024]{1,0:T(8,128)(2,1)S(1)}, u32[]{:S(2)}, u32[]{:S(2)}) collective-permute-start(bf16[96,1024]{1,0:T(8,128)(2,1)} %get-tuple-element.11), channel_id=1, source_target_pairs={{0,4},{2,6},{4,0},{6,2},{8,12},{10,14},{12,8},{14,10},{1,5},{3,7},... | collective-permute-start | bytes 589832 | tf_op jit(solution)/shard_map/ppermute | solution.py:44
  13.5 22.6 %collective-permute-start.2 = (bf16[96,1024]{1,0:T(8,128)(2,1)}, bf16[96,1024]{1,0:T(8,128)(2,1)S(1)}, u32[]{:S(2)}, u32[]{:S(2)}) collective-permute-start(bf16[96,1024]{1,0:T(8,128)(2,1)} %get-tuple-element.10), channel_id=1, source_target_pairs={{0,6},{2,4},{4,2},{6,0},{8,14},{10,12},{12,10},{14,8},{1,7},{3,5},... | collective-permute-start | bytes 589832 | tf_op jit(solution)/shard_map/ppermute | solution.py:44
  13.5 22.6 %collective-permute-start.3 = (bf16[96,1024]{1,0:T(8,128)(2,1)}, bf16[96,1024]{1,0:T(8,128)(2,1)S(1)}, u32[]{:S(2)}, u32[]{:S(2)}) collective-permute-start(bf16[96,1024]{1,0:T(8,128)(2,1)} %get-tuple-element.9), channel_id=1, source_target_pairs={{0,8},{2,10},{4,12},{6,14},{8,0},{10,2},{12,4},{14,6},{1,9},{3,11}... | collective-permute-start | bytes 589832 | tf_op jit(solution)/shard_map/ppermute | solution.py:44
  16.4 38.1 %collective-permute-start.4 = (bf16[96,1024]{1,0:T(8,128)(2,1)}, bf16[96,1024]{1,0:T(8,128)(2,1)S(1)}, u32[]{:S(2)}, u32[]{:S(2)}) collective-permute-start(bf16[96,1024]{1,0:T(8,128)(2,1)} %get-tuple-element.8), channel_id=1, source_target_pairs={{0,10},{2,8},{4,14},{6,12},{8,2},{10,0},{12,6},{14,4},{1,11},{3,9}... | collective-permute-start | bytes 589832 | tf_op jit(solution)/shard_map/ppermute | solution.py:44
  17.7 36.8 %collective-permute-start.5 = (bf16[96,1024]{1,0:T(8,128)(2,1)S(1)}, bf16[96,1024]{1,0:T(8,128)(2,1)S(1)}, u32[]{:S(2)}, u32[]{:S(2)}) collective-permute-start(bf16[96,1024]{1,0:T(8,128)(2,1)S(1)} %get-tuple-element.14), channel_id=1, source_target_pairs={{0,12},{2,14},{4,8},{6,10},{8,4},{10,6},{12,0},{14,2},{1,13},{3,15... | collective-permute-start | bytes 589832 | tf_op jit(solution)/shard_map/ppermute | solution.py:44
  31.5 25.8 %collective-permute-start.6 = (bf16[96,1024]{1,0:T(8,128)(2,1)S(1)}, bf16[96,1024]{1,0:T(8,128)(2,1)S(1)}, u32[]{:S(2)}, u32[]{:S(2)}) collective-permute-start(bf16[96,1024]{1,0:T(8,128)(2,1)S(1)} %get-tuple-element.7), channel_id=1, source_target_pairs={{0,14},{2,12},{4,10},{6,8},{8,6},{10,4},{12,2},{14,0},{1,15},{3,13... | collective-permute-start | bytes 589832 | tf_op jit(solution)/shard_map/ppermute | solution.py:44
  138.5 4.6 %copy-start = (bf16[1,4096,768]{2,1,0:T(8,128)(2,1)S(1)}, bf16[1,4096,768]{2,1,0:T(8,128)(2,1)}, u32[]{:S(2)}) copy-start(bf16[1,4096,768]{2,1,0:T(8,128)(2,1)} %all-gather.2.cloned.1.call-done) | copy-start | bytes 18874372
  184.0 0.7 copy-start.3
  184.0 116.6 %copy-start.1 = (bf16[1,512,768]{2,1,0:T(8,128)(2,1)S(1)}, bf16[1,512,768]{2,1,0:T(8,128)(2,1)}, u32[]{:S(2)}) copy-start(bf16[1,512,768]{2,1,0:T(8,128)(2,1)} %param.3) | copy-start | bytes 2359300
Sparse Core Ops, SparseCore 0:
  9.5 128.9 all-gather.1
  184.1 116.3 reduce-scatter.1
